TPU v7x, 32 devices: a whole 2x2x4 slice. The times are simulated.
32 devices in a mesh: pipe: 8 (over z, y), expert: 4 (over x, core).
Axes of the slice: x: 2, y: 2, z: 4, core: 2. Of those that a mesh axis runs over, the one named last changes fastest.
Arguments:
- first_input: bfloat16 [8, 256, 3072], P('pipe', 'expert'), may hold values from -6 to 6
- first_routes: int32 [8, 256, 2], P('pipe', 'expert'), may hold values from 0 to 7, as said below
- first_scores: float32 [8, 256, 2], P('pipe', 'expert'), may hold values from -6 to 6
- norm_gain: float32 [8, 3072], P('pipe'), may hold values from 0.5 to 1.5
- weight_in: bfloat16 [8, 2, 3072, 8192], P('pipe', None, None, 'expert'), may hold values from -0.109375 to 0.109375
- weight_out: bfloat16 [8, 8192, 3072], P('pipe', 'expert'), may hold values from -0.0625 to 0.0625
- second_grad: bfloat16 [8, 256, 3072], P('pipe', 'expert'), may hold values from -6 to 6
- second_routes: int32 [8, 256, 2], P('pipe', 'expert'), may hold values from 0 to 7, as said below
- second_scores: float32 [8, 256, 2], P('pipe', 'expert'), may hold values from -6 to 6
- second_stash: bfloat16 [8, 2, 80, 8192], P('pipe', None, None, 'expert'), may hold values from -5 to 5
Outputs:
- first_output: bfloat16 [8, 256, 3072], P('pipe', 'expert')
- input_grad: bfloat16 [8, 256, 3072], P('pipe', 'expert')
- mirror_stash: bfloat16 [8, 2, 80, 8192], P('pipe', None, None, 'expert')
Inputs may be any that keep to these rules, and one draw needn't show every extreme that they name: `first_routes`: each row names two different experts. At each section, the 64 rows of one index of the expert axis name expert 0 between 2 and 20 times, and at every section some index names it exactly 20 times. `second_routes`: as for first_routes.
All inputs are finite; a program needn't handle non-finite values.
Results may differ from a plain program's by a relative error of at most 0.0058.
Values may be sent and summed in bfloat16 or wider, within the bound.
No kernel may reach another device: no remote copies, remote signals or barrier semaphores. Data moves between devices by JAX's collectives and lax.ppermute only.
A program may use at most 128 MiB of HBM per device.

v0:
```python
import jax
import jax.numpy as jnp
from jax import lax
from jax.sharding import PartitionSpec as P

EPSILON = 1e-05


def partner(shard, axis, apart):
    return lax.ppermute(shard, axis, [(i, i ^ 1 << apart) for i in range(lax.axis_size(axis))])


def block_select(routes, scores, capacity):
    route_flags = (routes == 0).astype(jnp.int32)
    flag_line = route_flags.reshape(-1)
    earlier = (jnp.cumsum(flag_line) - flag_line).reshape(route_flags.shape)
    token_routed = jnp.sum(route_flags, axis=1)
    token_slot = jnp.sum(earlier * route_flags, axis=1) + (1 - token_routed) * capacity
    differ = scores[:, 0] - scores[:, 1]
    pair_weight = jnp.stack([jax.nn.sigmoid(differ), jax.nn.sigmoid(-differ)], axis=1)
    token_weight = jnp.sum(route_flags.astype(jnp.float32) * pair_weight, axis=1)
    selector = (jnp.arange(capacity, dtype=jnp.int32)[:, None] == token_slot[None, :]).astype(
        jnp.bfloat16
    )
    return (selector, token_weight)


def body(
    first_input,
    first_routes,
    first_scores,
    norm_gain,
    weight_in,
    weight_out,
    second_grad,
    second_routes,
    second_scores,
    second_stash,
):
    capacity = second_stash.shape[2] // lax.axis_size("expert")
    local_gate = weight_in[0, 0]
    local_up = weight_in[0, 1]
    local_out = weight_out[0]
    top_bit = lax.axis_size("pipe").bit_length() - 2
    along_rows = (((0,), (0,)), ((), ()))
    along_cols = (((1,), (1,)), ((), ()))
    fetched_early = partner(second_stash, "pipe", top_bit)
    wide_in = first_input[0].astype(jnp.float32)
    normed = (
        wide_in
        * lax.rsqrt(jnp.mean(wide_in * wide_in, axis=-1, keepdims=True) + EPSILON)
        * norm_gain[0]
    ).astype(jnp.bfloat16)
    first_select, first_weight = block_select(first_routes[0], first_scores[0], capacity)
    send_first = jnp.dot(first_select, normed, preferred_element_type=jnp.float32).astype(
        jnp.bfloat16
    )
    second_select, second_weight = block_select(second_routes[0], second_scores[0], capacity)
    scaled = (second_grad[0].astype(jnp.float32) * second_weight[:, None]).astype(jnp.bfloat16)
    send_second = jnp.dot(second_select, scaled, preferred_element_type=jnp.float32).astype(
        jnp.bfloat16
    )
    gathered_first = lax.all_gather(send_first, "expert", axis=0, tiled=True)
    gate_rows = jnp.dot(gathered_first, local_gate, preferred_element_type=jnp.float32)
    up_rows = jnp.dot(gathered_first, local_up, preferred_element_type=jnp.float32)
    stash_made = jnp.stack([gate_rows, up_rows]).astype(jnp.bfloat16)
    forward_hidden = (jax.nn.silu(gate_rows) * up_rows).astype(jnp.bfloat16)
    stash_made, hidden = (stash_made, forward_hidden)
    expert_out = lax.psum_scatter(
        jnp.dot(hidden, local_out, preferred_element_type=jnp.float32).astype(jnp.bfloat16),
        "expert",
        scatter_dimension=0,
        tiled=True,
    )
    mirror = partner(stash_made[None], "pipe", top_bit)
    stash_rows, mirror = (fetched_early[0], mirror)
    gathered_second = lax.all_gather(send_second, "expert", axis=0, tiled=True)
    grad_hidden = lax.dot_general(
        gathered_second, local_out, along_cols, preferred_element_type=jnp.float32
    )
    gate_part = stash_rows[0].astype(jnp.float32)
    up_part = stash_rows[1].astype(jnp.float32)
    sigmoid_gate = jax.nn.sigmoid(gate_part)
    swish_slope = sigmoid_gate * (1.0 + gate_part * (1.0 - sigmoid_gate))
    backward_grad_gate = (grad_hidden * up_part * swish_slope).astype(jnp.bfloat16)
    backward_grad_up = (grad_hidden * (gate_part * sigmoid_gate)).astype(jnp.bfloat16)
    grad_rows = lax.psum_scatter(
        lax.dot_general(
            backward_grad_gate, local_gate, along_cols, preferred_element_type=jnp.float32
        )
        + lax.dot_general(
            backward_grad_up, local_up, along_cols, preferred_element_type=jnp.float32
        ),
        "expert",
        scatter_dimension=0,
        tiled=True,
    ).astype(jnp.bfloat16)
    picked = lax.dot_general(
        first_select, expert_out, along_rows, preferred_element_type=jnp.float32
    )
    first_output = (wide_in + first_weight[:, None] * picked).astype(jnp.bfloat16)
    input_grad = lax.dot_general(
        second_select, grad_rows, along_rows, preferred_element_type=jnp.float32
    ).astype(jnp.bfloat16)
    return (first_output[None], input_grad[None], mirror)


def solution(mesh):
    placed = (
        P("pipe", "expert", None),
        P("pipe", "expert", None),
        P("pipe", "expert", None),
        P("pipe", None),
        P("pipe", None, None, "expert"),
        P("pipe", "expert", None),
        P("pipe", "expert", None),
        P("pipe", "expert", None),
        P("pipe", "expert", None),
        P("pipe", None, None, "expert"),
    )
    return jax.shard_map(
        body,
        mesh=mesh,
        in_specs=placed,
        out_specs=(
            P("pipe", "expert", None),
            P("pipe", "expert", None),
            P("pipe", None, None, "expert"),
        ),
        check_vma=False,
    )
```

profile of v0, /device:TPU:0, one launch (start us, length us, event | category | flops | bytes accessed | tf_op | source)
XLA Modules:
  0.0 98.6 jit_solution(2453879143578093232)
XLA Ops:
  0.6 4.1 %collective-permute-start = (bf16[1,2,80,2048]{3,2,1,0:T(8,128)(2,1)}, bf16[1,2,80,2048]{3,2,1,0:T(8,128)(2,1)}, u32[]{:S(2)}, u32[]{:S(2)}) collective-permute-start(bf16[1,2,80,2048]{3,2,1,0:T(8,128)(2,1)} %param.19), channel_id=1, source_target_pairs={{0,16},{4,20},{8,24},{12,28},{16,0},{20,4},{24,8},{28,12},{1,17},{... | collective-permute-start | bytes 1966088 | tf_op jit(solution)/shard_map/ppermute | solution.py:10
  4.8 0.7 fusion.78
  6.1 1.2 %fusion.30 = f32[64]{0:T(128)S(1)} fusion(bf16[1,64,3072]{2,1,0:T(8,128)(2,1)} %param.10), kind=kLoop, calls=%fused_computation.33 | loop fusion | flops 589760 | bytes 393472 | tf_op jit(solution)/shard_map/reduce_sum | solution.py:51
  7.4 1.3 %fusion.28 = bf16[1,20,3072]{2,1,0:T(8,128)(2,1)S(1)} fusion(bf16[1,64,3072]{2,1,0:T(8,128)(2,1)} %param.10, f32[3072]{0:T(1024)} %bitcast.109, f32[64]{0:T(128)S(1)} %add_rsqrt_fusion, s32[64]{0:T(128)S(1)} %multiply_add_fusion.1), kind=kOutput, calls=%fused_computation.26 | convolution fusion | flops 8713472 | bytes 528896 | tf_op jit(solution)/shard_map/dot_general | solution.py:55
  8.6 7.5 %all-gather = bf16[4,20,3072]{2,1,0:T(8,128)(2,1)S(1)} all-gather(bf16[1,20,3072]{2,1,0:T(8,128)(2,1)S(1)} %fusion.28), channel_id=1, replica_groups=mesh['pipe'=8,'expert'=4] {'expert'}, dimensions={0}, use_global_device_ids=true | all-gather | bytes 614400 | tf_op jit(solution)/shard_map/all_gather | solution.py:63
  16.3 6.0 %fusion.12 = f32[80,2048]{1,0:T(8,128)S(1)} fusion(bf16[80,3072]{1,0:T(8,128)(2,1)S(1)} %reshape.142, bf16[1,2,3072,2048]{3,2,1,0:T(8,128)(2,1)} %param.14), kind=kOutput, calls=%fused_computation.10 | convolution fusion | flops 1006632960 | bytes 13729792 | tf_op jit(solution)/shard_map/dot_general | solution.py:64
  22.3 6.0 %fusion.8 = f32[80,2048]{1,0:T(8,128)S(1)} fusion(bf16[80,3072]{1,0:T(8,128)(2,1)S(1)} %reshape.142, bf16[1,2,3072,2048]{3,2,1,0:T(8,128)(2,1)} %param.14), kind=kOutput, calls=%fused_computation.6 | convolution fusion | flops 1006632960 | bytes 13729792 | tf_op jit(solution)/shard_map/dot_general | solution.py:65
  28.4 2.4 %fusion.22 = bf16[80,3072]{1,0:T(8,128)(2,1)S(1)} fusion(bf16[1,2048,3072]{2,1,0:T(8,128)(2,1)S(1)} %bitcast.106, f32[80,2048]{1,0:T(8,128)S(1)} %fusion.8, f32[80,2048]{1,0:T(8,128)S(1)} %fusion.12), kind=kOutput, calls=%fused_computation.19 | convolution fusion | flops 1007861760 | bytes 14385152 | tf_op jit(solution)/shard_map/dot_general | solution.py:70
  30.8 11.3 %fusion = bf16[24,3072]{1,0:T(8,128)(2,1)S(1)} fusion(bf16[80,3072]{1,0:T(8,128)(2,1)S(1)} %fusion.22), kind=kCustom, calls=%all-reduce-scatter | all-reduce-scatter fusion | flops 294913 | bytes 639488
  42.1 1.3 %collective-permute-start.2 = (bf16[12,3072]{1,0:T(8,128)(2,1)S(1)}, bf16[12,3072]{1,0:T(8,128)(2,1)S(1)}, u32[]{:S(2)}, u32[]{:S(2)}) collective-permute-start(bf16[12,3072]{1,0:T(8,128)(2,1)S(1)} %slice.36), channel_id=1, source_target_pairs={{0,1},{1,2},{2,3},{4,5},{5,6},{6,7},{8,9},{9,10},{10,11},{12,13},{... | collective-permute-start | bytes 221192
  43.6 0.4 collective-permute-start.1
  45.0 8.4 %all-gather.1 = bf16[4,20,3072]{2,1,0:T(8,128)(2,1)S(1)} all-gather(bf16[1,20,3072]{2,1,0:T(8,128)(2,1)S(1)} %fusion.29), channel_id=1, replica_groups=mesh['pipe'=8,'expert'=4] {'expert'}, dimensions={0}, use_global_device_ids=true | all-gather | bytes 614400 | tf_op jit(solution)/shard_map/all_gather | solution.py:77
  53.6 0.6 dynamic-slice.6
  54.8 8.5 %fusion.2 = f32[80,2048]{1,0:T(8,128)S(1)} fusion(bf16[80,3072]{1,0:T(8,128)(2,1)S(1)} %reshape.144, bf16[1,2048,3072]{2,1,0:T(8,128)(2,1)} %param.15), kind=kOutput, calls=%fused_computation | convolution fusion | flops 1006632960 | bytes 13729792 | tf_op jit(solution)/shard_map/dot_general | solution.py:78
  63.4 0.4 concatenate.8
  63.7 0.4 copy-done.1
  64.2 6.9 %fusion.6 = f32[80,3072]{1,0:T(8,128)S(1)} fusion(bf16[1,2,3072,2048]{3,2,1,0:T(8,128)(2,1)} %param.14, f32[80,2048]{1,0:T(8,128)S(1)} %fusion.2, bf16[1,2,80,2048]{3,2,1,0:T(8,128)(2,1)} %collective-permute-done), kind=kOutput, calls=%fused_computation.4 | convolution fusion | flops 1007779840 | bytes 14548992 | tf_op jit(solution)/shard_map/dot_general | solution.py:91
  71.0 7.2 %fusion.18 = f32[80,3072]{1,0:T(8,128)S(1)} fusion(f32[80,3072]{1,0:T(8,128)S(1)} %fusion.6, bf16[1,2,3072,2048]{3,2,1,0:T(8,128)(2,1)} %param.14, f32[80,2048]{1,0:T(8,128)} %copy-done.1, bf16[1,2,80,2048]{3,2,1,0:T(8,128)(2,1)} %collective-permute-done), kind=kOutput, calls=%fused_computation.16 | convolution fusion | flops 1008844800 | bytes 15859712 | tf_op jit(solution)/shard_map/dot_general | solution.py:88
  78.3 15.6 %fusion.1 = f32[24,3072]{1,0:T(8,128)S(1)} fusion(f32[80,3072]{1,0:T(8,128)S(1)} %fusion.18), kind=kCustom, calls=%all-reduce-scatter.1 | all-reduce-scatter fusion | flops 294913 | bytes 1278464
  94.0 1.3 %collective-permute-start.3 = (bf16[12,3072]{1,0:T(8,128)(2,1)S(1)}, bf16[12,3072]{1,0:T(8,128)(2,1)S(1)}, u32[]{:S(2)}, u32[]{:S(2)}) collective-permute-start(bf16[12,3072]{1,0:T(8,128)(2,1)S(1)} %slice.37), channel_id=1, source_target_pairs={{0,1},{1,2},{2,3},{4,5},{5,6},{6,7},{8,9},{9,10},{10,11},{12,13},{... | collective-permute-start | bytes 221192
  95.3 1.1 %fusion.26 = bf16[1,64,3072]{2,1,0:T(8,128)(2,1)} fusion(bf16[1,64,3072]{2,1,0:T(8,128)(2,1)S(1)} %copy-done, f32[64]{0:T(128)S(1)} %fusion.71, bf16[36,3072]{1,0:T(8,128)(2,1)S(1)} %concatenate.8, u32[]{:S(6)} %subtract, s32[64]{0:T(128)S(1)} %multiply_add_fusion.1), kind=kOutput, calls=%fused_computation.22 | convolution fusion | flops 8652032 | bytes 934916 | tf_op jit(solution)/shard_map/dot_general | solution.py:98
  96.3 0.3 concatenate.9
  96.7 1.1 %fusion.27 = bf16[1,64,3072]{2,1,0:T(8,128)(2,1)} fusion(bf16[36,3072]{1,0:T(8,128)(2,1)S(1)} %concatenate.9, u32[]{:S(6)} %subtract, s32[64]{0:T(128)S(1)} %multiply_add_fusion), kind=kOutput, calls=%fused_computation.23 | convolution fusion | flops 8062208 | bytes 541188 | tf_op jit(solution)/shard_map/dot_general | solution.py:102
  97.8 0.8 copy.32
  (53 shorter events, 2.3 us)
Async XLA Ops:
  0.6 63.1 %collective-permute-start = (bf16[1,2,80,2048]{3,2,1,0:T(8,128)(2,1)}, bf16[1,2,80,2048]{3,2,1,0:T(8,128)(2,1)}, u32[]{:S(2)}, u32[]{:S(2)}) collective-permute-start(bf16[1,2,80,2048]{3,2,1,0:T(8,128)(2,1)} %param.19), channel_id=1, source_target_pairs={{0,16},{4,20},{8,24},{12,28},{16,0},{20,4},{24,8},{28,12},{1,17},{... | collective-permute-start | bytes 1966088 | tf_op jit(solution)/shard_map/ppermute | solution.py:10
  16.3 12.0 %slice-start = ((s8[12582912]{0:T(1024)(128)(4,1)}), s8[4194304]{0:T(1024)(128)(4,1)S(1)}, s32[]{:S(2)}) async-start(s8[12582912]{0:T(1024)(128)(4,1)} %bitcast.105), calls=%async_computation | async-start | bytes 8388608
  16.3 12.0 %slice-start.1 = ((s8[12582912]{0:T(1024)(128)(4,1)}), s8[4194304]{0:T(1024)(128)(4,1)S(1)}, s32[]{:S(2)}) async-start(s8[12582912]{0:T(1024)(128)(4,1)} %bitcast.105), calls=%async_computation.1 | async-start | bytes 8388608
  22.3 6.1 %slice-start.2 = ((s8[12582912]{0:T(1024)(128)(4,1)}), s8[4194304]{0:T(1024)(128)(4,1)S(1)}, s32[]{:S(2)}) async-start(s8[12582912]{0:T(1024)(128)(4,1)} %bitcast.105), calls=%async_computation.2 | async-start | bytes 8388608
  28.4 15.6 %copy-start.3 = (s32[1,64,2]{1,2,0:T(2,128)S(1)}, s32[1,64,2]{1,2,0:T(2,128)}, u32[]{:S(2)}) copy-start(s32[1,64,2]{1,2,0:T(2,128)} %param.17) | copy-start | bytes 1540
  28.4 16.3 %copy-start.4 = (f32[1,64,2]{1,2,0:T(2,128)S(1)}, f32[1,64,2]{1,2,0:T(2,128)}, u32[]{:S(2)}) copy-start(f32[1,64,2]{1,2,0:T(2,128)} %param.18) | copy-start | bytes 1540
  28.4 16.4 %copy-start.2 = (bf16[1,64,3072]{2,1,0:T(8,128)(2,1)S(1)}, bf16[1,64,3072]{2,1,0:T(8,128)(2,1)}, u32[]{:S(2)}) copy-start(bf16[1,64,3072]{2,1,0:T(8,128)(2,1)} %param.16) | copy-start | bytes 1179652
  28.4 25.1 %copy-start.5 = (f32[1,64,2]{1,2,0:T(2,128)S(1)}, f32[1,64,2]{1,2,0:T(2,128)}, u32[]{:S(2)}) copy-start(f32[1,64,2]{1,2,0:T(2,128)} %param.12) | copy-start | bytes 1540
  28.4 25.2 %copy-start.6 = (u32[32]{0:T(128)S(1)}, u32[32]{0:T(128)}, u32[]{:S(2)}) copy-start(u32[32]{0:T(128)} %constant.37) | copy-start | bytes 388
  42.1 21.2 %collective-permute-start.2 = (bf16[12,3072]{1,0:T(8,128)(2,1)S(1)}, bf16[12,3072]{1,0:T(8,128)(2,1)S(1)}, u32[]{:S(2)}, u32[]{:S(2)}) collective-permute-start(bf16[12,3072]{1,0:T(8,128)(2,1)S(1)} %slice.36), channel_id=1, source_target_pairs={{0,1},{1,2},{2,3},{4,5},{5,6},{6,7},{8,9},{9,10},{10,11},{12,13},{... | collective-permute-start | bytes 221192
  43.6 52.8 %collective-permute-start.1 = (bf16[1,2,80,2048]{3,2,1,0:T(8,128)(2,1)S(1)}, bf16[1,2,80,2048]{3,2,1,0:T(8,128)(2,1)S(1)}, u32[]{:S(2)}, u32[]{:S(2)}) collective-permute-start(bf16[1,2,80,2048]{3,2,1,0:T(8,128)(2,1)S(1)} %pad_maximum_fusion), channel_id=1, source_target_pairs={{0,16},{4,20},{8,24},{12,28},{16,0},{20,4},{24,8},{28,12},{1,17},{... | collective-permute-start | bytes 1966088 | tf_op jit(solution)/shard_map/ppermute | solution.py:10
  63.3 0.8 copy-start.1
  71.0 24.2 %copy-start = (bf16[1,64,3072]{2,1,0:T(8,128)(2,1)S(1)}, bf16[1,64,3072]{2,1,0:T(8,128)(2,1)}, u32[]{:S(2)}) copy-start(bf16[1,64,3072]{2,1,0:T(8,128)(2,1)} %param.10) | copy-start | bytes 1179652
  94.0 2.4 %collective-permute-start.3 = (bf16[12,3072]{1,0:T(8,128)(2,1)S(1)}, bf16[12,3072]{1,0:T(8,128)(2,1)S(1)}, u32[]{:S(2)}, u32[]{:S(2)}) collective-permute-start(bf16[12,3072]{1,0:T(8,128)(2,1)S(1)} %slice.37), channel_id=1, source_target_pairs={{0,1},{1,2},{2,3},{4,5},{5,6},{6,7},{8,9},{9,10},{10,11},{12,13},{... | collective-permute-start | bytes 221192
where the time goes:
time: 100 us; the launch traced here: 98.6 us
  blocking collectives  42.9 us (43%)
  matrix products  40.6 us (41%)
  starting transfers between devices  7.12 us (7%)
  local copies, waits for them, and re-layouts  3.68 us (4%)
  other arithmetic  2.72 us (3%)
  between operations  1.61 us (2%)
    unnamed x2, blocking collectives  26.9 us
    dot_general x1, matrix products, body(): lax.dot_general(gathered_second, local_out, along_cols, preferred_element...  8.5 us
    all_gather x1, blocking collectives, body(): gathered_second = lax.all_gather(send_second, 'expert', axis=0, tiled=True)  8.4 us
    all_gather x1, blocking collectives, body(): gathered_first = lax.all_gather(send_first, 'expert', axis=0, tiled=True)  7.53 us
    dot_general x1, matrix products, body(): lax.dot_general(backward_grad_gate, local_gate, along_cols, preferred_ele...  7.24 us
    dot_general x1, matrix products, body(): lax.dot_general(backward_grad_up, local_up, along_cols, preferred_element...  6.87 us
    dot_general x1, matrix products, body(): jnp.dot(gathered_first, local_up, preferred_element_type=jnp.float32)  5.98 us
    dot_general x1, matrix products, body(): jnp.dot(gathered_first, local_gate, preferred_element_type=jnp.float32)  5.98 us
  transfers between devices with their start and end apart: 4, of which 0 were waited for; matrix products, arithmetic and copies ran while one was open for 72% of the time, Pallas kernels for 0%

commit v1 on v0

v1 whole, which is shorter than its diff:
```python
import jax
import jax.numpy as jnp
from jax import lax
from jax.sharding import PartitionSpec as P

EPSILON = 1e-05
F32 = jnp.float32
BF16 = jnp.bfloat16


def partner(shard, axis, apart):
    return lax.ppermute(shard, axis, [(i, i ^ (1 << apart)) for i in range(lax.axis_size(axis))])


def bits_of(axis):
    return lax.axis_size(axis).bit_length() - 1


def gather_blocks(block, axis):
    me = lax.axis_index(axis)
    held = block
    for bit in reversed(range(bits_of(axis))):
        other = partner(held, axis, bit)
        mine_low = (me >> bit) & 1 == 0
        held = jnp.stack([jnp.where(mine_low, held, other), jnp.where(mine_low, other, held)], axis=1)
        held = held.reshape((-1,) + block.shape[1:])
    return held


def scatter_blocks(parts, axis):
    me = lax.axis_index(axis)
    held = parts
    for bit in range(bits_of(axis)):
        split = held.reshape((-1, 2) + held.shape[1:])
        mine = (me >> bit) & 1
        keep = lax.dynamic_index_in_dim(split, mine, 1, keepdims=False)
        send = lax.dynamic_index_in_dim(split, 1 - mine, 1, keepdims=False)
        held = keep + partner(send.astype(BF16), axis, bit).astype(F32)
    return held


def block_select(routes, scores, capacity):
    routed = jnp.any(routes == 0, axis=1)
    tokens = routes.shape[0]
    step = jnp.arange(tokens, dtype=jnp.int32)
    before = (step[:, None] < step[None, :]) & routed[:, None]
    slot = jnp.sum(before.astype(jnp.int32), axis=0)
    slot = jnp.where(routed, slot, capacity)
    differ = scores[:, 0] - scores[:, 1]
    weight = jnp.where(
        routes[:, 0] == 0, jax.nn.sigmoid(differ), jnp.where(routes[:, 1] == 0, jax.nn.sigmoid(-differ), 0.0)
    )
    selector = (jnp.arange(capacity, dtype=jnp.int32)[:, None] == slot[None, :]).astype(BF16)
    return (selector, weight)


def body(
    first_input,
    first_routes,
    first_scores,
    norm_gain,
    weight_in,
    weight_out,
    second_grad,
    second_routes,
    second_scores,
    second_stash,
):
    size = lax.axis_size("expert")
    capacity = second_stash.shape[2] // size
    local_gate = weight_in[0, 0]
    local_up = weight_in[0, 1]
    local_out = weight_out[0]
    width = first_input.shape[2]
    top_bit = bits_of("pipe") - 1
    along_rows = (((0,), (0,)), ((), ()))
    along_cols = (((1,), (1,)), ((), ()))
    fetched = partner(second_stash, "pipe", top_bit)
    wide_in = first_input[0].astype(F32)
    normed = (
        wide_in * lax.rsqrt(jnp.mean(wide_in * wide_in, axis=-1, keepdims=True) + EPSILON) * norm_gain[0]
    ).astype(BF16)
    first_select, first_weight = block_select(first_routes[0], first_scores[0], capacity)
    second_select, second_weight = block_select(second_routes[0], second_scores[0], capacity)
    send_first = jnp.dot(first_select, normed, preferred_element_type=F32).astype(BF16)
    scaled = (second_grad[0].astype(F32) * second_weight[:, None]).astype(BF16)
    send_second = jnp.dot(second_select, scaled, preferred_element_type=F32).astype(BF16)

    rows = gather_blocks(send_first[None], "expert").reshape(-1, width)
    rows_second = gather_blocks(send_second[None], "expert").reshape(-1, width)
    gate_rows = jnp.dot(rows, local_gate, preferred_element_type=F32)
    up_rows = jnp.dot(rows, local_up, preferred_element_type=F32)
    stash_made = jnp.stack([gate_rows, up_rows]).astype(BF16)
    mirror = partner(stash_made[None], "pipe", top_bit)
    hidden = (jax.nn.silu(gate_rows) * up_rows).astype(BF16)
    out_part = jnp.dot(hidden, local_out, preferred_element_type=F32)
    expert_out = scatter_blocks(out_part.reshape(size, capacity, width), "expert")[0].astype(BF16)

    grad_hidden = lax.dot_general(rows_second, local_out, along_cols, preferred_element_type=F32)
    gate_part = fetched[0, 0].astype(F32)
    up_part = fetched[0, 1].astype(F32)
    sigmoid_gate = jax.nn.sigmoid(gate_part)
    swish_slope = sigmoid_gate * (1.0 + gate_part * (1.0 - sigmoid_gate))
    grad_gate = (grad_hidden * up_part * swish_slope).astype(BF16)
    grad_up = (grad_hidden * (gate_part * sigmoid_gate)).astype(BF16)
    grad_part = lax.dot_general(grad_gate, local_gate, along_cols, preferred_element_type=F32) + lax.dot_general(
        grad_up, local_up, along_cols, preferred_element_type=F32
    )
    grad_rows = scatter_blocks(grad_part.reshape(size, capacity, width), "expert")[0].astype(BF16)

    picked = lax.dot_general(first_select, expert_out, along_rows, preferred_element_type=F32)
    first_output = (wide_in + first_weight[:, None] * picked).astype(BF16)
    input_grad = lax.dot_general(second_select, grad_rows, along_rows, preferred_element_type=F32).astype(BF16)
    return (first_output[None], input_grad[None], mirror)


def solution(mesh):
    tokens = P("pipe", "expert", None)
    columns = P("pipe", None, None, "expert")
    return jax.shard_map(
        body,
        mesh=mesh,
        in_specs=(
            tokens,
            tokens,
            tokens,
            P("pipe", None),
            columns,
            tokens,
            tokens,
            tokens,
            tokens,
            columns,
        ),
        out_specs=(tokens, tokens, columns),
        check_vma=False,
    )
```

time: 100 us -> 83.7 us (0.84)
  blocking collectives: 42.9 us -> 0 us
  waiting for transfers between devices: 0.01 us -> 18.1 us
  matrix products: 40.6 us -> 46.8 us
  other arithmetic: 2.72 us -> 5.71 us
  starting transfers between devices: 7.12 us -> 8.31 us
    unnamed x2 -> x0, blocking collectives: 26.9 us -> none
    ppermute x2 -> x10, waiting for transfers between devices: 0.01 us -> 18.1 us  [partner(): lax.ppermute(shard, axis, [(i, i ^ 1 << apart) for i in range(lax.axis_si...]
    all_gather x2 -> x0, blocking collectives: 15.9 us -> none  [the longest x1 8.4 us: body(): gathered_second = lax.all_gather(send_second, 'expert', axis=0, tiled=True)]
    dot_general x8, matrix products: 38.4 us -> 44.6 us  [the longest x1 8.51 us: body(): lax.dot_general(rows_second, local_out, along_cols, preferred_element_typ...]
    ppermute x2 -> x10, starting transfers between devices: 4.53 us -> 8.31 us  [partner(): lax.ppermute(shard, axis, [(i, i ^ 1 << apart) for i in range(lax.axis_si...]
    unnamed x2 -> x0, starting transfers between devices: 2.59 us -> none
    mul x0 -> x2, other arithmetic: none -> 1.54 us  [the longest x1 0.77 us: body(): scaled = (second_grad[0].astype(F32) * second_weight[:, None]).astype(BF16)]
    reduce_or x0 -> x2, other arithmetic: none -> 1.4 us  [block_select(): routed = jnp.any(routes == 0, axis=1)]
  transfers between devices with their start and end apart: 4 -> 10, of which waited for: 0 -> 6; matrix products, arithmetic and copies ran while one was open for 72% -> 60% of each run, Pallas kernels for 0% -> 0%
where the time goes in v1:
time: 83.7 us; the launch traced here: 83.2 us
  matrix products  46.8 us (56%)
  waiting for transfers between devices  18.1 us (22%)
  starting transfers between devices  8.31 us (10%)
  other arithmetic  5.71 us (7%)
  local copies, waits for them, and re-layouts  3.41 us (4%)
  between operations  0.89 us (1%)
    ppermute x10, waiting for transfers between devices, partner(): lax.ppermute(shard, axis, [(i, i ^ 1 << apart) for i in range(lax.axis_si...  18.1 us
    dot_general x1, matrix products, body(): lax.dot_general(rows_second, local_out, along_cols, preferred_element_typ...  8.51 us
    ppermute x10, starting transfers between devices, partner(): lax.ppermute(shard, axis, [(i, i ^ 1 << apart) for i in range(lax.axis_si...  8.31 us
    dot_general x1, matrix products, body(): lax.dot_general(grad_gate, local_gate, along_cols, preferred_element_type...  7.09 us
    dot_general x1, matrix products, body(): gate_rows = jnp.dot(rows, local_gate, preferred_element_type=F32)  7.02 us
    dot_general x1, matrix products, body(): lax.dot_general(grad_up, local_up, along_cols, preferred_element_type=F32)  6.89 us
    dot_general x1, matrix products, body(): out_part = jnp.dot(hidden, local_out, preferred_element_type=F32)  6.74 us
    dot_general x1, matrix products, body(): up_rows = jnp.dot(rows, local_up, preferred_element_type=F32)  5.85 us
  transfers between devices with their start and end apart: 10, of which 6 were waited for; matrix products, arithmetic and copies ran while one was open for 60% of the time, Pallas kernels for 0%

profile of v1, /device:TPU:0, one launch (start us, length us, event | category | flops | bytes accessed | tf_op | source)
XLA Modules:
  0.0 83.2 jit_solution(17191612573319730649)
XLA Ops:
  1.4 0.8 fusion.64
  2.2 1.3 %fusion.24 = bf16[1,20,3072]{2,1,0:T(8,128)(2,1)S(1)} fusion(bf16[1,64,3072]{2,1,0:T(8,128)(2,1)} %param.16, f32[64]{0:T(128)S(1)} %fusion.64, s32[64]{0:T(128)S(1)} %broadcast_select_fusion), kind=kOutput, calls=%fused_computation.26 | convolution fusion | flops 8516864 | bytes 516608 | tf_op jit(solution)/shard_map/dot_general | solution.py:87
  3.5 3.0 %collective-permute-start.4 = (bf16[1,20,3072]{2,1,0:T(8,128)(2,1)S(1)}, bf16[1,20,3072]{2,1,0:T(8,128)(2,1)S(1)}, u32[]{:S(2)}, u32[]{:S(2)}) collective-permute-start(bf16[1,20,3072]{2,1,0:T(8,128)(2,1)S(1)} %fusion.24), channel_id=1, source_target_pairs={{0,2},{1,3},{2,0},{3,1},{4,6},{5,7},{6,4},{7,5},{8,10},{9,11},{10,... | collective-permute-start | bytes 368648 | tf_op jit(solution)/shard_map/ppermute | solution.py:12
  6.5 2.6 %collective-permute-start.6 = (bf16[1,2,80,2048]{3,2,1,0:T(8,128)(2,1)}, bf16[1,2,80,2048]{3,2,1,0:T(8,128)(2,1)S(1)}, u32[]{:S(2)}, u32[]{:S(2)}) collective-permute-start(bf16[1,2,80,2048]{3,2,1,0:T(8,128)(2,1)} %param.19), channel_id=1, source_target_pairs={{0,16},{4,20},{8,24},{12,28},{16,0},{20,4},{24,8},{28,12},{1,17},{... | collective-permute-start | bytes 1966088 | tf_op jit(solution)/shard_map/ppermute | solution.py:12
  9.9 1.2 %fusion.25 = f32[64]{0:T(128)S(1)} fusion(bf16[1,64,3072]{2,1,0:T(8,128)(2,1)} %param.10), kind=kLoop, calls=%fused_computation.32 | loop fusion | flops 589760 | bytes 393472 | tf_op jit(solution)/shard_map/reduce_sum | solution.py:81
  11.1 1.3 %fusion.23 = bf16[1,20,3072]{2,1,0:T(8,128)(2,1)S(1)} fusion(bf16[1,64,3072]{2,1,0:T(8,128)(2,1)} %param.10, f32[3072]{0:T(1024)} %bitcast.125, f32[64]{0:T(128)S(1)} %add_rsqrt_fusion, s32[64]{0:T(128)S(1)} %broadcast_select_fusion.1), kind=kOutput, calls=%fused_computation.25 | convolution fusion | flops 8713472 | bytes 528896 | tf_op jit(solution)/shard_map/dot_general | solution.py:85
  13.0 0.8 fusion.63
  13.9 3.7 %collective-permute-done = bf16[1,20,3072]{2,1,0:T(8,128)(2,1)S(1)} collective-permute-done((bf16[1,20,3072]{2,1,0:T(8,128)(2,1)S(1)}, bf16[1,20,3072]{2,1,0:T(8,128)(2,1)S(1)}, u32[]{:S(2)}, u32[]{:S(2)}) %collective-permute-start) | collective-permute-done | bytes 122912 | tf_op jit(solution)/shard_map/ppermute | solution.py:12
  18.0 1.3 %collective-permute-done.1 = bf16[2,20,3072]{2,1,0:T(8,128)(2,1)S(1)} collective-permute-done((bf16[2,20,3072]{2,1,0:T(8,128)(2,1)S(1)}, bf16[2,20,3072]{2,1,0:T(8,128)(2,1)S(1)}, u32[]{:S(2)}, u32[]{:S(2)}) %collective-permute-start.1) | collective-permute-done | bytes 245792 | tf_op jit(solution)/shard_map/ppermute | solution.py:12
  19.6 5.9 %fusion.6 = f32[80,2048]{1,0:T(8,128)S(1)} fusion(bf16[80,3072]{1,0:T(8,128)(2,1)S(1)} %reshape_reshape.10, bf16[1,2,3072,2048]{3,2,1,0:T(8,128)(2,1)} %param.14), kind=kOutput, calls=%fused_computation.6 | convolution fusion | flops 1006632960 | bytes 13729792 | tf_op jit(solution)/shard_map/dot_general | solution.py:92
  25.5 7.0 %convert_bitcast_fusion.1 = (bf16[1,1,80,2048]{3,2,1,0:T(8,128)(2,1)S(1)}, bf16[80,2048]{1,0:T(8,128)(2,1)S(1)}, bf16[1,1,80,2048]{3,2,1,0:T(8,128)(2,1)S(1)}) fusion(f32[80,2048]{1,0:T(8,128)S(1)} %fusion.6, bf16[80,3072]{1,0:T(8,128)(2,1)S(1)} %reshape_reshape.10, bf16[1,2,3072,2048]{3,2,1,0:T(8,128)(2,1)} %param.14), kind=kOutput, calls=%fused_computation.63 | convolution fusion | flops 1007943680 | bytes 14712832 | tf_op jit(solution)/shard_map/dot_general | solution.py:91
  32.6 6.7 %fusion = f32[2,2,20,3072]{3,2,1,0:T(8,128)S(1)} fusion(bf16[2,2,20,2048]{3,2,1,0:T(8,128)(2,1)S(1)} %dot_general.35, bf16[1,2048,3072]{2,1,0:T(8,128)(2,1)} %param.15), kind=kOutput, calls=%fused_computation | convolution fusion | flops 1006632960 | bytes 13893632 | tf_op jit(solution)/shard_map/dot_general | solution.py:96
  39.6 8.5 %fusion.2 = f32[80,2048]{1,0:T(8,128)S(1)} fusion(bf16[80,3072]{1,0:T(8,128)(2,1)S(1)} %reshape_reshape.11, bf16[1,2048,3072]{2,1,0:T(8,128)(2,1)} %param.15), kind=kOutput, calls=%fused_computation.2 | convolution fusion | flops 1006632960 | bytes 13729792 | tf_op jit(solution)/shard_map/dot_general | solution.py:99
  48.1 0.9 %pad_maximum_fusion = bf16[1,2,80,2048]{3,2,1,0:T(8,128)(2,1)} fusion(bf16[1,1,80,2048]{3,2,1,0:T(8,128)(2,1)S(1)} %get-tuple-element.5, bf16[1,1,80,2048]{3,2,1,0:T(8,128)(2,1)S(1)} %get-tuple-element.3), kind=kLoop, calls=%fused_computation.46 | loop fusion | flops 327680 | bytes 1310720 | tf_op jit(solution)/shard_map/stack | solution.py:93
  49.4 0.8 copy-done.1
  50.2 6.9 %fusion.4 = f32[80,3072]{1,0:T(8,128)S(1)} fusion(bf16[1,2,3072,2048]{3,2,1,0:T(8,128)(2,1)} %param.14, f32[80,2048]{1,0:T(8,128)S(1)} %fusion.2, bf16[1,2,80,2048]{3,2,1,0:T(8,128)(2,1)S(1)} %collective-permute-done.6), kind=kOutput, calls=%fused_computation.4 | convolution fusion | flops 1007779840 | bytes 14548992 | tf_op jit(solution)/shard_map/dot_general | solution.py:106
  57.1 7.1 %fusion.16 = f32[80,3072]{1,0:T(8,128)S(1)} fusion(f32[80,3072]{1,0:T(8,128)S(1)} %fusion.4, bf16[1,2,3072,2048]{3,2,1,0:T(8,128)(2,1)} %param.14, f32[80,2048]{1,0:T(8,128)S(1)} %fusion.2, bf16[1,2,80,2048]{3,2,1,0:T(8,128)(2,1)} %copy-done.1), kind=kOutput, calls=%fused_computation.16 | convolution fusion | flops 1008844800 | bytes 15859712 | tf_op jit(solution)/shard_map/dot_general | solution.py:106
  65.1 0.9 %collective-permute-done.7 = bf16[2,20,3072]{2,1,0:T(8,128)(2,1)S(1)} collective-permute-done((bf16[2,20,3072]{2,1,0:T(8,128)(2,1)S(1)}, bf16[2,20,3072]{2,1,0:T(8,128)(2,1)S(1)}, u32[]{:S(2)}, u32[]{:S(2)}) %collective-permute-start.7) | collective-permute-done | bytes 245792 | tf_op jit(solution)/shard_map/ppermute | solution.py:12
  66.8 4.5 %collective-permute-done.3 = bf16[1,20,3072]{2,1,0:T(8,128)(2,1)S(1)} collective-permute-done((bf16[1,20,3072]{2,1,0:T(8,128)(2,1)S(1)}, bf16[1,20,3072]{2,1,0:T(8,128)(2,1)S(1)}, u32[]{:S(2)}, u32[]{:S(2)}) %collective-permute-start.3) | collective-permute-done | bytes 122912 | tf_op jit(solution)/shard_map/ppermute | solution.py:12
  71.4 1.1 %fusion.21 = bf16[1,64,3072]{2,1,0:T(8,128)(2,1)} fusion(bf16[1,64,3072]{2,1,0:T(8,128)(2,1)S(1)} %copy-done, f32[64]{0:T(128)S(1)} %fusion.63, bf16[1,20,3072]{2,1,0:T(8,128)(2,1)S(1)} %collective-permute-done.3, f32[2,20,3072]{2,1,0:T(8,128)S(1)} %bitcast_add_fusion.1, s32[]{:T(128)S(6)} %select_n.102, s32[64]{0:T(128)S(1)} %broadcast_select_fusion.1), kind=kOutput, calls=%fused_computation.21 | convolution fusion | flops 8836352 | bytes 1229828 | tf_op jit(solution)/shard_map/dot_general | solution.py:111
  72.4 1.5 %collective-permute-done.8 = bf16[1,20,3072]{2,1,0:T(8,128)(2,1)S(1)} collective-permute-done((bf16[1,20,3072]{2,1,0:T(8,128)(2,1)S(1)}, bf16[1,20,3072]{2,1,0:T(8,128)(2,1)S(1)}, u32[]{:S(2)}, u32[]{:S(2)}) %collective-permute-start.8) | collective-permute-done | bytes 122912 | tf_op jit(solution)/shard_map/ppermute | solution.py:12
  74.0 1.1 %fusion.22 = bf16[1,64,3072]{2,1,0:T(8,128)(2,1)} fusion(bf16[1,20,3072]{2,1,0:T(8,128)(2,1)S(1)} %collective-permute-done.8, f32[2,20,3072]{2,1,0:T(8,128)S(1)} %bitcast_add_fusion, s32[]{:T(128)S(6)} %select_n.102, s32[64]{0:T(128)S(1)} %broadcast_select_fusion), kind=kOutput, calls=%fused_computation.22 | convolution fusion | flops 8246528 | bytes 836100 | tf_op jit(solution)/shard_map/dot_general | solution.py:113
  75.0 6.2 %collective-permute-done.9 = bf16[1,2,80,2048]{3,2,1,0:T(8,128)(2,1)} collective-permute-done((bf16[1,2,80,2048]{3,2,1,0:T(8,128)(2,1)}, bf16[1,2,80,2048]{3,2,1,0:T(8,128)(2,1)}, u32[]{:S(2)}, u32[]{:S(2)}) %collective-permute-start.9) | collective-permute-done | bytes 655392 | tf_op jit(solution)/shard_map/ppermute | solution.py:12
  81.2 2.0 %copy.19 = bf16[1,2,80,2048]{3,2,1,0:T(8,128)(2,1)} copy(bf16[1,2,80,2048]{3,2,1,0:T(8,128)(2,1)} %collective-permute-done.9) | data formatting | bytes 1310720
  (42 shorter events, 5.4 us)
Async XLA Ops:
  3.5 10.3 %collective-permute-start.4 = (bf16[1,20,3072]{2,1,0:T(8,128)(2,1)S(1)}, bf16[1,20,3072]{2,1,0:T(8,128)(2,1)S(1)}, u32[]{:S(2)}, u32[]{:S(2)}) collective-permute-start(bf16[1,20,3072]{2,1,0:T(8,128)(2,1)S(1)} %fusion.24), channel_id=1, source_target_pairs={{0,2},{1,3},{2,0},{3,1},{4,6},{5,7},{6,4},{7,5},{8,10},{9,11},{10,... | collective-permute-start | bytes 368648 | tf_op jit(solution)/shard_map/ppermute | solution.py:12
  6.5 42.9 %collective-permute-start.6 = (bf16[1,2,80,2048]{3,2,1,0:T(8,128)(2,1)}, bf16[1,2,80,2048]{3,2,1,0:T(8,128)(2,1)S(1)}, u32[]{:S(2)}, u32[]{:S(2)}) collective-permute-start(bf16[1,2,80,2048]{3,2,1,0:T(8,128)(2,1)} %param.19), channel_id=1, source_target_pairs={{0,16},{4,20},{8,24},{12,28},{16,0},{20,4},{24,8},{28,12},{1,17},{... | collective-permute-start | bytes 1966088 | tf_op jit(solution)/shard_map/ppermute | solution.py:12
  12.4 5.2 %collective-permute-start = (bf16[1,20,3072]{2,1,0:T(8,128)(2,1)S(1)}, bf16[1,20,3072]{2,1,0:T(8,128)(2,1)S(1)}, u32[]{:S(2)}, u32[]{:S(2)}) collective-permute-start(bf16[1,20,3072]{2,1,0:T(8,128)(2,1)S(1)} %fusion.23), channel_id=1, source_target_pairs={{0,2},{1,3},{2,0},{3,1},{4,6},{5,7},{6,4},{7,5},{8,10},{9,11},{10,... | collective-permute-start | bytes 368648 | tf_op jit(solution)/shard_map/ppermute | solution.py:12
  13.8 3.9 %collective-permute-start.5 = (bf16[2,20,3072]{2,1,0:T(8,128)(2,1)S(1)}, bf16[2,20,3072]{2,1,0:T(8,128)(2,1)S(1)}, u32[]{:S(2)}, u32[]{:S(2)}) collective-permute-start(bf16[2,20,3072]{2,1,0:T(8,128)(2,1)S(1)} %maximum_bitcast_fusion.1), channel_id=1, source_target_pairs={{0,1},{1,0},{2,3},{3,2},{4,5},{5,4},{6,7},{7,6},{8,9},{9,8},{10,11... | collective-permute-start | bytes 737288 | tf_op jit(solution)/shard_map/ppermute | solution.py:12
  17.7 1.6 %collective-permute-start.1 = (bf16[2,20,3072]{2,1,0:T(8,128)(2,1)S(1)}, bf16[2,20,3072]{2,1,0:T(8,128)(2,1)S(1)}, u32[]{:S(2)}, u32[]{:S(2)}) collective-permute-start(bf16[2,20,3072]{2,1,0:T(8,128)(2,1)S(1)} %maximum_bitcast_fusion), channel_id=1, source_target_pairs={{0,1},{1,0},{2,3},{3,2},{4,5},{5,4},{6,7},{7,6},{8,9},{9,8},{10,11... | collective-permute-start | bytes 737288 | tf_op jit(solution)/shard_map/ppermute | solution.py:12
  39.4 10.0 %collective-permute-start.2 = (bf16[2,20,3072]{2,1,0:T(8,128)(2,1)S(1)}, bf16[2,20,3072]{2,1,0:T(8,128)(2,1)S(1)}, u32[]{:S(2)}, u32[]{:S(2)}) collective-permute-start(bf16[2,20,3072]{2,1,0:T(8,128)(2,1)S(1)} %fusion.49), channel_id=1, source_target_pairs={{0,1},{1,0},{2,3},{3,2},{4,5},{5,4},{6,7},{7,6},{8,9},{9,8},{10,11... | collective-permute-start | bytes 737288 | tf_op jit(solution)/shard_map/ppermute | solution.py:12
  49.0 32.3 %collective-permute-start.9 = (bf16[1,2,80,2048]{3,2,1,0:T(8,128)(2,1)}, bf16[1,2,80,2048]{3,2,1,0:T(8,128)(2,1)}, u32[]{:S(2)}, u32[]{:S(2)}) collective-permute-start(bf16[1,2,80,2048]{3,2,1,0:T(8,128)(2,1)} %pad_maximum_fusion), channel_id=1, source_target_pairs={{0,16},{4,20},{8,24},{12,28},{16,0},{20,4},{24,8},{28,12},{1,17},{... | collective-permute-start | bytes 1966088 | tf_op jit(solution)/shard_map/ppermute | solution.py:12
  49.4 0.8 %copy-start.1 = (bf16[1,2,80,2048]{3,2,1,0:T(8,128)(2,1)}, bf16[1,2,80,2048]{3,2,1,0:T(8,128)(2,1)S(1)}, u32[]{:S(2)}) copy-start(bf16[1,2,80,2048]{3,2,1,0:T(8,128)(2,1)S(1)} %collective-permute-done.6) | copy-start | bytes 1966084
  57.1 14.2 %copy-start = (bf16[1,64,3072]{2,1,0:T(8,128)(2,1)S(1)}, bf16[1,64,3072]{2,1,0:T(8,128)(2,1)}, u32[]{:S(2)}) copy-start(bf16[1,64,3072]{2,1,0:T(8,128)(2,1)} %param.10) | copy-start | bytes 1179652
  64.4 1.6 %collective-permute-start.7 = (bf16[2,20,3072]{2,1,0:T(8,128)(2,1)S(1)}, bf16[2,20,3072]{2,1,0:T(8,128)(2,1)S(1)}, u32[]{:S(2)}, u32[]{:S(2)}) collective-permute-start(bf16[2,20,3072]{2,1,0:T(8,128)(2,1)S(1)} %fusion.50), channel_id=1, source_target_pairs={{0,1},{1,0},{2,3},{3,2},{4,5},{5,4},{6,7},{7,6},{8,9},{9,8},{10,11... | collective-permute-start | bytes 737288 | tf_op jit(solution)/shard_map/ppermute | solution.py:12
  64.6 6.8 %collective-permute-start.3 = (bf16[1,20,3072]{2,1,0:T(8,128)(2,1)S(1)}, bf16[1,20,3072]{2,1,0:T(8,128)(2,1)S(1)}, u32[]{:S(2)}, u32[]{:S(2)}) collective-permute-start(bf16[1,20,3072]{2,1,0:T(8,128)(2,1)S(1)} %dynamic-slice_convert_fusion.3), channel_id=1, source_target_pairs={{0,2},{1,3},{2,0},{3,1},{4,6},{5,7},{6,4},{7,5},{8,10},{9,11},{10,... | collective-permute-start | bytes 368648 | tf_op jit(solution)/shard_map/ppermute | solution.py:12
  66.1 7.8 %collective-permute-start.8 = (bf16[1,20,3072]{2,1,0:T(8,128)(2,1)S(1)}, bf16[1,20,3072]{2,1,0:T(8,128)(2,1)S(1)}, u32[]{:S(2)}, u32[]{:S(2)}) collective-permute-start(bf16[1,20,3072]{2,1,0:T(8,128)(2,1)S(1)} %dynamic-slice_convert_fusion.2), channel_id=1, source_target_pairs={{0,2},{1,3},{2,0},{3,1},{4,6},{5,7},{6,4},{7,5},{8,10},{9,11},{10,... | collective-permute-start | bytes 368648 | tf_op jit(solution)/shard_map/ppermute | solution.py:12

commit v2 on v1

v2 whole, which is shorter than its diff:
```python
import functools

import jax
import jax.numpy as jnp
from jax import lax
from jax.experimental import pallas as pl
from jax.experimental.pallas import tpu as pltpu
from jax.sharding import PartitionSpec as P

EPSILON = 1e-05
F32 = jnp.float32
BF16 = jnp.bfloat16
I32 = jnp.int32
ALONG_ROWS = (((0,), (0,)), ((), ()))
ALONG_COLS = (((1,), (1,)), ((), ()))
VMEM = pl.BlockSpec(memory_space=pltpu.VMEM)
SMEM = pl.BlockSpec(memory_space=pltpu.SMEM)


def dot(a, b, dims=None):
    return lax.dot_general(a, b, dims or (((1,), (0,)), ((), ())), preferred_element_type=F32)


def partner(shard, axis, apart):
    return lax.ppermute(shard, axis, [(i, i ^ (1 << apart)) for i in range(lax.axis_size(axis))])


def bits_of(axis):
    return lax.axis_size(axis).bit_length() - 1


def tile_of(length, most):
    return max(t for t in range(128, min(length, most) + 1, 128) if length % t == 0)


def gather_blocks(block, axis):
    me = lax.axis_index(axis)
    held = block
    for bit in reversed(range(bits_of(axis))):
        other = partner(held, axis, bit)
        mine_low = (me >> bit) & 1 == 0
        held = jnp.stack([jnp.where(mine_low, held, other), jnp.where(mine_low, other, held)], axis=1)
        held = held.reshape((-1,) + block.shape[1:])
    return held


def scatter_rest(held, axis, first_bit):
    me = lax.axis_index(axis)
    for bit in range(first_bit, bits_of(axis)):
        split = held.reshape((-1, 2) + held.shape[1:])
        mine = (me >> bit) & 1
        keep = lax.dynamic_index_in_dim(split, mine, 1, keepdims=False)
        send = lax.dynamic_index_in_dim(split, 1 - mine, 1, keepdims=False)
        held = keep.astype(F32) + partner(send.astype(BF16), axis, bit).astype(F32)
    return held


def block_select(routes, scores, capacity):
    routed = jnp.any(routes == 0, axis=1)
    tokens = routes.shape[0]
    step = jnp.arange(tokens, dtype=I32)
    before = (step[:, None] < step[None, :]) & routed[:, None]
    slot = jnp.where(routed, jnp.sum(before.astype(I32), axis=0), capacity)
    differ = scores[:, 0] - scores[:, 1]
    weight = jnp.where(
        routes[:, 0] == 0, jax.nn.sigmoid(differ), jnp.where(routes[:, 1] == 0, jax.nn.sigmoid(-differ), 0.0)
    )
    selector = (jnp.arange(capacity, dtype=I32)[:, None] == slot[None, :]).astype(BF16)
    return (selector, weight)


def selector_of(routes, capacity):
    tokens = routes.shape[0]
    routed = jnp.max((routes == 0).astype(F32), axis=1, keepdims=True)
    row = lax.broadcasted_iota(I32, (tokens, tokens), 0)
    col = lax.broadcasted_iota(I32, (tokens, tokens), 1)
    slot = jnp.sum(jnp.where(row < col, routed, 0.0), axis=0, keepdims=True)
    here = jnp.sum(jnp.where(row == col, routed, 0.0), axis=0, keepdims=True)
    slot = jnp.where(here > 0.0, slot, float(capacity)).astype(I32)
    return jnp.where(lax.broadcasted_iota(I32, (capacity, tokens), 0) == slot, 1.0, 0.0).astype(BF16)


def packing(counts, base, blocks, capacity, early, spill, late_only=False, early_only=False):
    head = blocks * early
    first = head if late_only else 0
    rows = (head if early_only else head + spill) - first
    row = lax.broadcasted_iota(I32, (rows, blocks * capacity), 0) + first
    col = lax.broadcasted_iota(I32, (rows, blocks * capacity), 1)
    hit = None
    offset = head
    for s in range(blocks):
        slot = col - s * capacity
        tests = []
        if not late_only:
            tests.append((slot >= 0) & (slot < early) & (row == s * early + slot))
        if not early_only:
            count = counts[base + s]
            tests.append((slot >= early) & (slot < count) & (row == slot + (offset - early)) & (row >= head))
            offset = offset + jnp.maximum(count - early, 0)
        for test in tests:
            hit = test if hit is None else hit | test
    return jnp.where(hit, 1.0, 0.0).astype(BF16)


def store_split(value, keep_ref, send_ref, parity, capacity, columns):
    blocks = value.shape[0] // capacity
    for s in range(blocks):
        block = value[s * capacity : (s + 1) * capacity]

        @pl.when(parity == s % 2)
        def _():
            keep_ref[s // 2, :, columns] = block

        @pl.when(parity != s % 2)
        def _():
            send_ref[s // 2, :, columns] = block


def early_kernel(blocks, capacity, early, spill, stash_ref, out_ref):
    pick = packing(None, 0, blocks, capacity, early, spill, early_only=True)
    for g in range(2):
        out_ref[g] = dot(pick, stash_ref[g]).astype(BF16)


def late_kernel(blocks, capacity, early, spill, counts_ref, stash_ref, out_ref):
    pick = packing(counts_ref, 3 * blocks, blocks, capacity, early, spill, late_only=True)
    for g in range(2):
        out_ref[g] = dot(pick, stash_ref[g]).astype(BF16)


def first_kernel(input_ref, gain_ref, routes_ref, second_routes_ref, out_ref, counts_ref):
    wide = input_ref[...].astype(F32)
    scale = lax.rsqrt(jnp.mean(wide * wide, axis=-1, keepdims=True) + EPSILON)
    normed = (wide * scale * gain_ref[...]).astype(BF16)
    out_ref[...] = dot(selector_of(routes_ref[...], out_ref.shape[0]), normed).astype(BF16)
    counts_ref[0:1, :] = jnp.broadcast_to(jnp.sum((routes_ref[...] == 0).astype(I32)), (1, counts_ref.shape[1]))
    counts_ref[1:2, :] = jnp.broadcast_to(
        jnp.sum((second_routes_ref[...] == 0).astype(I32)), (1, counts_ref.shape[1])
    )


def second_kernel(grad_ref, routes_ref, scores_ref, out_ref):
    routes = routes_ref[...]
    differ = scores_ref[:, 0:1] - scores_ref[:, 1:2]
    weight = jnp.where(
        routes[:, 0:1] == 0, jax.nn.sigmoid(differ), jnp.where(routes[:, 1:2] == 0, jax.nn.sigmoid(-differ), 0.0)
    )
    scaled = (grad_ref[...].astype(F32) * weight).astype(BF16)
    out_ref[...] = dot(selector_of(routes, out_ref.shape[0]), scaled).astype(BF16)


def gate_up_kernel(blocks, capacity, early, spill, counts_ref, rows_ref, weight_ref, packed_ref, hidden_ref, pick_ref):
    @pl.when(pl.program_id(0) == 0)
    def _():
        pick_ref[...] = packing(counts_ref, 0, blocks, capacity, early, spill)

    rows = rows_ref[...]
    gate = dot(rows, weight_ref[0])
    up = dot(rows, weight_ref[1])
    hidden_ref[...] = (gate * jax.nn.sigmoid(gate) * up).astype(BF16)
    packed_ref[0] = dot(pick_ref[...], gate.astype(BF16)).astype(BF16)
    packed_ref[1] = dot(pick_ref[...], up.astype(BF16)).astype(BF16)


def out_kernel(
    blocks,
    capacity,
    early,
    spill,
    counts_ref,
    hidden_ref,
    rows_ref,
    weight_ref,
    keep_ref,
    send_ref,
    grad_hidden_ref,
    total_ref,
    packed_ref,
):
    step = pl.program_id(0)

    @pl.when(step == 0)
    def _():
        pick = packing(counts_ref, blocks, blocks, capacity, early, spill)
        packed_ref[...] = dot(pick, rows_ref[...]).astype(BF16)
        total_ref[...] = jnp.zeros_like(total_ref)

    weight = weight_ref[...]
    grad_hidden_ref[...] = dot(packed_ref[...], weight, ALONG_COLS)
    total_ref[...] += dot(hidden_ref[...], weight)

    @pl.when(step == pl.num_programs(0) - 1)
    def _():
        store_split(total_ref[...].astype(BF16), keep_ref, send_ref, counts_ref[4 * blocks] % 2, capacity, slice(None))


def grads_kernel(
    blocks,
    capacity,
    early,
    spill,
    counts_ref,
    early_ref,
    late_ref,
    grad_hidden_ref,
    weight_ref,
    keep_ref,
    send_ref,
    grad_gate_ref,
    grad_up_ref,
    pick_ref,
):
    @pl.when(pl.program_id(0) == 0)
    def _():
        pick_ref[...] = packing(counts_ref, blocks, blocks, capacity, early, spill)
        head = blocks * early
        for part, rows in ((early_ref, slice(0, head)), (late_ref, slice(head, head + spill))):
            gate = part[0].astype(F32)
            up = part[1].astype(F32)
            grad_hidden = grad_hidden_ref[rows]
            q = jax.nn.sigmoid(gate)
            grad_gate_ref[rows] = (grad_hidden * up * (q * (1.0 + gate * (1.0 - q)))).astype(BF16)
            grad_up_ref[rows] = (grad_hidden * (gate * q)).astype(BF16)

    part = dot(grad_gate_ref[...], weight_ref[0], ALONG_COLS) + dot(grad_up_ref[...], weight_ref[1], ALONG_COLS)
    rows = dot(pick_ref[...], part.astype(BF16), ALONG_ROWS).astype(BF16)
    store_split(rows, keep_ref, send_ref, counts_ref[4 * blocks] % 2, capacity, slice(None))


def unpack_kernel(blocks, capacity, early, spill, counts_ref, packed_ref, out_ref):
    pick = packing(counts_ref, 2 * blocks, blocks, capacity, early, spill)
    out_ref[...] = dot(pick, packed_ref[...], ALONG_ROWS).astype(BF16)


def body(
    first_input,
    first_routes,
    first_scores,
    norm_gain,
    weight_in,
    weight_out,
    second_grad,
    second_routes,
    second_scores,
    second_stash,
):
    blocks = lax.axis_size("expert")
    me = lax.axis_index("expert")
    rows_all, units = second_stash.shape[2:]
    width = first_input.shape[2]
    capacity = rows_all // blocks
    early = capacity * 2 // 5
    spill = blocks * early
    packed_rows = blocks * early + spill
    plan = (blocks, capacity, early, spill)
    top_bit = bits_of("pipe") - 1
    stash_in = second_stash[0]
    weights_in = weight_in[0]
    weights_out = weight_out[0]

    early_rows = pl.pallas_call(
        functools.partial(early_kernel, *plan),
        out_shape=jax.ShapeDtypeStruct((2, blocks * early, units), BF16),
        in_specs=[VMEM],
        out_specs=VMEM,
        name="pack_early",
    )(stash_in)
    fetched_early = partner(early_rows, "pipe", top_bit)

    send_first, counts = pl.pallas_call(
        first_kernel,
        out_shape=(
            jax.ShapeDtypeStruct((capacity, width), BF16),
            jax.ShapeDtypeStruct((2, blocks), I32),
        ),
        in_specs=[VMEM] * 4,
        out_specs=(VMEM, VMEM),
        name="select_first",
    )(first_input[0], norm_gain, first_routes[0], second_routes[0])
    mine = jnp.where(jnp.arange(blocks, dtype=I32)[None, :] == me, counts, 0)
    tally = jnp.stack([mine, partner(mine, "pipe", top_bit)])
    for bit in reversed(range(bits_of("expert"))):
        tally = tally + partner(tally, "expert", bit)
    info = jnp.concatenate([tally.reshape(-1), me.astype(I32)[None]])
    send_second = pl.pallas_call(
        second_kernel,
        out_shape=jax.ShapeDtypeStruct((capacity, width), BF16),
        in_specs=[VMEM] * 3,
        out_specs=VMEM,
        name="select_second",
    )(second_grad[0], second_routes[0], second_scores[0])
    rows = gather_blocks(send_first[None], "expert").reshape(-1, width)
    rows_second = gather_blocks(send_second[None], "expert").reshape(-1, width)

    late_rows = pl.pallas_call(
        functools.partial(late_kernel, *plan),
        out_shape=jax.ShapeDtypeStruct((2, spill, units), BF16),
        in_specs=[SMEM, VMEM],
        out_specs=VMEM,
        name="pack_late",
    )(info, stash_in)
    fetched_late = partner(late_rows, "pipe", top_bit)

    over = jnp.max(jnp.sum(jnp.maximum(tally - early, 0), axis=-1) - spill).reshape(1)
    for bit in range(top_bit):
        over = jnp.maximum(over, partner(over, "pipe", bit))

    tile = tile_of(units, 256)
    packed, hidden = pl.pallas_call(
        functools.partial(gate_up_kernel, *plan),
        grid=(units // tile,),
        out_shape=(
            jax.ShapeDtypeStruct((2, packed_rows, units), BF16),
            jax.ShapeDtypeStruct((rows_all, units), BF16),
        ),
        in_specs=[
            SMEM,
            pl.BlockSpec((rows_all, width), lambda i: (0, 0)),
            pl.BlockSpec((2, width, tile), lambda i: (0, 0, i)),
        ],
        out_specs=(
            pl.BlockSpec((2, packed_rows, tile), lambda i: (0, 0, i)),
            pl.BlockSpec((rows_all, tile), lambda i: (0, i)),
        ),
        scratch_shapes=[pltpu.VMEM((packed_rows, rows_all), BF16)],
        cost_estimate=pl.CostEstimate(
            flops=4 * rows_all * width * units, bytes_accessed=4 * width * units, transcendentals=0
        ),
        name="gate_up",
    )(info, rows, weights_in)
    mirror_packed = partner(packed, "pipe", top_bit)

    tile = tile_of(units, 256)
    half = (blocks // 2, capacity, width)
    whole = lambda shape: pl.BlockSpec(shape, lambda i: (0,) * len(shape))
    out_keep, out_send, grad_hidden = pl.pallas_call(
        functools.partial(out_kernel, *plan),
        grid=(units // tile,),
        out_shape=(
            jax.ShapeDtypeStruct(half, BF16),
            jax.ShapeDtypeStruct(half, BF16),
            jax.ShapeDtypeStruct((packed_rows, units), F32),
        ),
        in_specs=[
            SMEM,
            pl.BlockSpec((rows_all, tile), lambda i: (0, i)),
            whole((rows_all, width)),
            pl.BlockSpec((tile, width), lambda i: (i, 0)),
        ],
        out_specs=(whole(half), whole(half), pl.BlockSpec((packed_rows, tile), lambda i: (0, i))),
        scratch_shapes=[pltpu.VMEM((rows_all, width), F32), pltpu.VMEM((packed_rows, width), BF16)],
        cost_estimate=pl.CostEstimate(
            flops=4 * rows_all * width * units, bytes_accessed=2 * width * units, transcendentals=0
        ),
        name="out_and_grad_hidden",
    )(info, hidden, rows_second, weights_out)
    expert_out = scatter_rest(
        out_keep.astype(F32) + partner(out_send, "expert", 0).astype(F32), "expert", 1
    )[0].astype(BF16)
    first_select, first_weight = block_select(first_routes[0], first_scores[0], capacity)
    picked = dot(first_select, expert_out, ALONG_ROWS)
    first_output = (first_input[0].astype(F32) + first_weight[:, None] * picked).astype(BF16)

    tile = tile_of(width, 384)
    split = pl.BlockSpec((blocks // 2, capacity, tile), lambda i: (0, 0, i))
    grad_keep, grad_send = pl.pallas_call(
        functools.partial(grads_kernel, *plan),
        grid=(width // tile,),
        out_shape=(jax.ShapeDtypeStruct(half, BF16), jax.ShapeDtypeStruct(half, BF16)),
        in_specs=[
            SMEM,
            whole((2, blocks * early, units)),
            whole((2, spill, units)),
            whole((packed_rows, units)),
            pl.BlockSpec((2, tile, units), lambda i: (0, i, 0)),
        ],
        out_specs=(split, split),
        scratch_shapes=[
            pltpu.VMEM((packed_rows, units), BF16),
            pltpu.VMEM((packed_rows, units), BF16),
            pltpu.VMEM((packed_rows, rows_all), BF16),
        ],
        cost_estimate=pl.CostEstimate(
            flops=4 * packed_rows * width * units, bytes_accessed=4 * width * units, transcendentals=0
        ),
        name="grads",
    )(info, fetched_early, fetched_late, grad_hidden, weights_in)
    grad_rows = scatter_rest(
        grad_keep.astype(F32) + partner(grad_send, "expert", 0).astype(F32), "expert", 1
    )[0].astype(BF16)
    second_select, _ = block_select(second_routes[0], second_scores[0], capacity)

    def packed_case(grad_rows, packed, info):
        tile = tile_of(units, 1024)
        mirror = pl.pallas_call(
            functools.partial(unpack_kernel, *plan),
            grid=(2, units // tile),
            out_shape=jax.ShapeDtypeStruct((2, rows_all, units), BF16),
            in_specs=[SMEM, pl.BlockSpec((None, packed_rows, tile), lambda g, i: (g, 0, i))],
            out_specs=pl.BlockSpec((None, rows_all, tile), lambda g, i: (g, 0, i)),
            name="unpack",
        )(info, packed)
        return (dot(second_select, grad_rows, ALONG_ROWS).astype(BF16)[None], mirror[None])

    def full_case(grad_rows, packed, info):
        fetched = partner(stash_in, "pipe", top_bit)
        gate = dot(rows, weights_in[0])
        up = dot(rows, weights_in[1])
        mirror = partner(jnp.stack([gate, up]).astype(BF16), "pipe", top_bit)
        grad_hidden = dot(rows_second, weights_out, ALONG_COLS)
        gate = fetched[0].astype(F32)
        up = fetched[1].astype(F32)
        q = jax.nn.sigmoid(gate)
        grad_gate = (grad_hidden * up * (q * (1.0 + gate * (1.0 - q)))).astype(BF16)
        grad_up = (grad_hidden * (gate * q)).astype(BF16)
        parts = dot(grad_gate, weights_in[0], ALONG_COLS) + dot(grad_up, weights_in[1], ALONG_COLS)
        full_rows = scatter_rest(parts.reshape(blocks, capacity, width), "expert", 0)[0].astype(BF16)
        return (dot(second_select, full_rows, ALONG_ROWS).astype(BF16)[None], mirror[None])

    input_grad, mirror = lax.cond(over[0] > 0, full_case, packed_case, grad_rows, mirror_packed, info)
    return (first_output[None], input_grad, mirror)


def solution(mesh):
    tokens = P("pipe", "expert", None)
    columns = P("pipe", None, None, "expert")
    return jax.shard_map(
        body,
        mesh=mesh,
        in_specs=(
            tokens,
            tokens,
            tokens,
            P("pipe", None),
            columns,
            tokens,
            tokens,
            tokens,
            tokens,
            columns,
        ),
        out_specs=(tokens, tokens, columns),
        check_vma=False,
    )
```

time: 83.7 us -> 112 us (1.34)
  Pallas kernels: 0 us -> 52.7 us
  matrix products: 46.8 us -> 2.29 us
  starting transfers between devices: 8.31 us -> 18.9 us
  local copies, waits for them, and re-layouts: 3.41 us -> 9.39 us
  other arithmetic: 5.71 us -> 7.87 us
  between operations: 0.89 us -> 2.69 us
  waiting for transfers between devices: 18.1 us -> 16.6 us
    pallas_call x0 -> x8, Pallas kernels: none -> 52.7 us  [the longest x1 15.7 us: body(): pl.pallas_call(functools.partial(grads_kernel, *plan), grid=(width // til...]
    dot_general x10 -> x2, matrix products: 46.8 us -> 2.29 us  [dot(): lax.dot_general(a, b, dims or (((1,), (0,)), ((), ())), preferred_element...]
    ppermute x10 -> x16, starting transfers between devices: 8.31 us -> 18.9 us  [partner(): lax.ppermute(shard, axis, [(i, i ^ 1 << apart) for i in range(lax.axis_si...]
    squeeze x0 -> x3, local copies, waits for them, and re-layouts: none -> 4.13 us  [the longest x1 1.38 us: body(): first_routes[0]]
    another operation x6, other arithmetic: 0.29 us -> 2.11 us  [gather_blocks(): jnp.stack([jnp.where(mine_low, held, other), jnp.where(mine_low, other, h...]
    ppermute x10 -> x16, waiting for transfers between devices: 18.1 us -> 16.6 us  [partner(): lax.ppermute(shard, axis, [(i, i ^ 1 << apart) for i in range(lax.axis_si...]
    convert_element_type x4 -> x2, local copies, waits for them, and re-layouts: 0.12 us -> 1.37 us  [scatter_rest(): held = keep.astype(F32) + partner(send.astype(BF16), axis, bit).astype(F32)]
    unnamed x5 -> x13, local copies, waits for them, and re-layouts: 2.82 us -> 3.51 us
  transfers between devices with their start and end apart: 10 -> 16, of which waited for: 6 -> 6; matrix products, arithmetic and copies ran while one was open for 60% -> 11% of each run, Pallas kernels for 0% -> 42%
where the time goes in v2:
time: 112 us; the launch traced here: 110 us
  Pallas kernels  52.7 us (47%)
  starting transfers between devices  18.9 us (17%)
  waiting for transfers between devices  16.6 us (15%)
  local copies, waits for them, and re-layouts  9.39 us (8%)
  other arithmetic  7.87 us (7%)
  between operations  2.69 us (2%)
  matrix products  2.29 us (2%)
    ppermute x16, starting transfers between devices, partner(): lax.ppermute(shard, axis, [(i, i ^ 1 << apart) for i in range(lax.axis_si...  18.9 us
    ppermute x16, waiting for transfers between devices, partner(): lax.ppermute(shard, axis, [(i, i ^ 1 << apart) for i in range(lax.axis_si...  16.6 us
    pallas_call x1, Pallas kernels, body(): pl.pallas_call(functools.partial(grads_kernel, *plan), grid=(width // til...  15.7 us
    pallas_call x1, Pallas kernels, body(): pl.pallas_call(functools.partial(gate_up_kernel, *plan), grid=(units // t...  13.2 us
    pallas_call x1, Pallas kernels, body(): pl.pallas_call(functools.partial(out_kernel, *plan), grid=(units // tile,...  11.8 us
    pallas_call x1, Pallas kernels, packed_case(): pl.pallas_call(functools.partial(unpack_kernel, *plan), grid=(2, units //...  3.74 us
    unnamed x13, local copies, waits for them, and re-layouts  3.51 us
    dot_general x2, matrix products, dot(): lax.dot_general(a, b, dims or (((1,), (0,)), ((), ())), preferred_element...  2.29 us
  transfers between devices with their start and end apart: 16, of which 6 were waited for; matrix products, arithmetic and copies ran while one was open for 11% of the time, Pallas kernels for 42%

profile of v2, /device:TPU:0, one launch (start us, length us, event | category | flops | bytes accessed | tf_op | source)
XLA Modules:
  0.0 110.4 jit_solution(14905395106686581123)
XLA Ops:
  0.6 1.4 %copy.24.routes_ref = s32[64,2]{1,0:T(8,128)} copy(s32[64,2]{0,1:T(2,128)} %bitcast.139) | data formatting | bytes 1024 | tf_op jit(solution)/shard_map/squeeze | solution.py:360
  2.0 1.4 %copy.25.second_routes_ref.routes_ref = s32[64,2]{1,0:T(8,128)} copy(s32[64,2]{0,1:T(2,128)} %bitcast.142) | data formatting | bytes 1024 | tf_op jit(solution)/shard_map/squeeze | solution.py:279
  3.4 2.0 %select_first.1 = (bf16[20,3072]{1,0:T(8,128)(2,1)}, s32[2,4]{1,0:T(2,128)}) custom-call(bf16[64,3072]{1,0:T(8,128)(2,1)} %bitcast.132, f32[1,3072]{1,0:T(1,128)} %gain_ref.1, s32[64,2]{1,0:T(8,128)} %copy.24.routes_ref, s32[64,2]{1,0:T(8,128)} %copy.25.second_routes_ref.routes_ref), custom_call_target="tpu_custom_call" | custom-call | tf_op jit(solution)/shard_map/select_first/pallas_call | solution.py:270
  6.1 4.1 %collective-permute-start.4 = (s32[2,4]{1,0:T(2,128)S(1)}, s32[2,4]{1,0:T(2,128)S(1)}, u32[]{:S(2)}, u32[]{:S(2)}) collective-permute-start(s32[2,4]{1,0:T(2,128)S(1)} %broadcast_select_fusion), channel_id=1, source_target_pairs={{0,16},{4,20},{8,24},{12,28},{16,0},{20,4},{24,8},{28,12},{1,17},{... | collective-permute-start | bytes 104 | tf_op jit(solution)/shard_map/ppermute | solution.py:25
  10.2 1.5 %collective-permute-start.7 = (bf16[1,20,3072]{2,1,0:T(8,128)(2,1)}, bf16[1,20,3072]{2,1,0:T(8,128)(2,1)S(1)}, u32[]{:S(2)}, u32[]{:S(2)}) collective-permute-start(bf16[1,20,3072]{2,1,0:T(8,128)(2,1)} %bitcast.135), channel_id=1, source_target_pairs={{0,2},{1,3},{2,0},{3,1},{4,6},{5,7},{6,4},{7,5},{8,10},{9,11},{10,... | collective-permute-start | bytes 368648 | tf_op jit(solution)/shard_map/ppermute | solution.py:25
  11.6 1.4 %copy.28.scores_ref = f32[64,2]{1,0:T(8,128)} copy(f32[64,2]{0,1:T(2,128)} %bitcast.141) | data formatting | bytes 1024 | tf_op jit(solution)/shard_map/squeeze | solution.py:291
  13.0 2.2 %select_second.1 = bf16[20,3072]{1,0:T(8,128)(2,1)} custom-call(bf16[64,3072]{1,0:T(8,128)(2,1)} %bitcast.134, s32[64,2]{1,0:T(8,128)} %copy.25.second_routes_ref.routes_ref, f32[64,2]{1,0:T(8,128)} %copy.28.scores_ref), custom_call_target="tpu_custom_call" | custom-call | tf_op jit(solution)/shard_map/select_second/pallas_call | solution.py:285
  15.7 2.0 %pack_early.1 = bf16[2,32,2048]{2,1,0:T(8,128)(2,1)} custom-call(bf16[2,80,2048]{2,1,0:T(8,128)(2,1)} %bitcast.129), custom_call_target="tpu_custom_call" | custom-call | tf_op jit(solution)/shard_map/pack_early/pallas_call | solution.py:261
  20.7 1.9 %collective-permute-start.5 = (s32[2,2,4]{2,1,0:T(2,128)S(1)}, s32[2,2,4]{2,1,0:T(2,128)S(1)}, u32[]{:S(2)}, u32[]{:S(2)}) collective-permute-start(s32[2,2,4]{2,1,0:T(2,128)S(1)} %pad_add_fusion), channel_id=1, source_target_pairs={{0,2},{1,3},{2,0},{3,1},{4,6},{5,7},{6,4},{7,5},{8,10},{9,11},{10,... | collective-permute-start | bytes 200 | tf_op jit(solution)/shard_map/ppermute | solution.py:25
  22.6 1.8 %collective-permute-done.5 = s32[2,2,4]{2,1,0:T(2,128)S(1)} collective-permute-done((s32[2,2,4]{2,1,0:T(2,128)S(1)}, s32[2,2,4]{2,1,0:T(2,128)S(1)}, u32[]{:S(2)}, u32[]{:S(2)}) %collective-permute-start.5) | collective-permute-done | bytes 96 | tf_op jit(solution)/shard_map/ppermute | solution.py:25
  25.8 2.0 %pack_late.1 = bf16[2,32,2048]{2,1,0:T(8,128)(2,1)} custom-call(s32[17]{0:T(128)S(1)} %pad_add_fusion.1.counts_ref, bf16[2,80,2048]{2,1,0:T(8,128)(2,1)} %bitcast.130), custom_call_target="tpu_custom_call" | custom-call | tf_op jit(solution)/shard_map/pack_late/pallas_call | solution.py:295
  27.8 2.9 %collective-permute-start.16 = (bf16[2,32,2048]{2,1,0:T(8,128)(2,1)}, bf16[2,32,2048]{2,1,0:T(8,128)(2,1)S(1)}, u32[]{:S(2)}, u32[]{:S(2)}) collective-permute-start(bf16[2,32,2048]{2,1,0:T(8,128)(2,1)} %pack_late.1), channel_id=1, source_target_pairs={{0,16},{4,20},{8,24},{12,28},{16,0},{20,4},{24,8},{28,12},{1,17},{... | collective-permute-start | bytes 786440 | tf_op jit(solution)/shard_map/ppermute | solution.py:25
  34.9 13.2 %gate_up.1 = (bf16[2,64,2048]{2,1,0:T(8,128)(2,1)}, bf16[80,2048]{1,0:T(8,128)(2,1)}) custom-call(s32[17]{0:T(128)S(1)} %pad_add_fusion.1.counts_ref, bf16[80,3072]{1,0:T(8,128)(2,1)S(1)} %reshape_reshape.6.rows_ref, bf16[2,3072,2048]{2,1,0:T(8,128)(2,1)} %bitcast.124), custom_call_target="tpu_custom_call" | custom-call | flops 2013265920 | bytes 25165824 | tf_op jit(solution)/shard_map/gate_up/pallas_call | solution.py:309
  48.1 11.8 %out_and_grad_hidden.1 = (bf16[2,20,3072]{2,1,0:T(8,128)(2,1)}, bf16[2,20,3072]{2,1,0:T(8,128)(2,1)}, f32[64,2048]{1,0:T(8,128)}) custom-call(s32[17]{0:T(128)S(1)} %pad_add_fusion.1.counts_ref, bf16[80,2048]{1,0:T(8,128)(2,1)} %get-tuple-element.57.hidden_ref, bf16[80,3072]{1,0:T(8,128)(2,1)S(1)} %reshape_reshape.7.rows_ref, bf16[2048,3072]{1,0:T(8,128)(2,1)} %bitcast.127), custom_call_target="tpu_custom_call" | custom-call | flops 2013265920 | bytes 12582912 | tf_op jit(solution)/shard_map/out_and_grad_hidden/pallas_call | solution.py:336
  61.7 15.7 %grads.1 = (bf16[2,20,3072]{2,1,0:T(8,128)(2,1)}, bf16[2,20,3072]{2,1,0:T(8,128)(2,1)}) custom-call(s32[17]{0:T(128)S(1)} %pad_add_fusion.1.counts_ref, bf16[2,32,2048]{2,1,0:T(8,128)(2,1)} %copy-done.6, bf16[2,32,2048]{2,1,0:T(8,128)(2,1)} %copy-done.7, f32[64,2048]{1,0:T(8,128)} %get-tuple-element.60.grad_hidden_ref, bf16[2,3072,2048]{2,1,0:T(8,128)(2,1)} %bitcast.125), custom_call_target="tpu_custom_call" | custom-call | flops 1610612736 | bytes 25165824 | tf_op jit(solution)/shard_map/grads/pallas_call | solution.py:366
  78.4 1.8 %collective-permute-start.12 = (bf16[1,20,3072]{2,1,0:T(8,128)(2,1)}, bf16[1,20,3072]{2,1,0:T(8,128)(2,1)}, u32[]{:S(2)}, u32[]{:S(2)}) collective-permute-start(bf16[1,20,3072]{2,1,0:T(8,128)(2,1)} %dynamic-slice_convert_fusion.3), channel_id=1, source_target_pairs={{0,2},{1,3},{2,0},{3,1},{4,6},{5,7},{6,4},{7,5},{8,10},{9,11},{10,... | collective-permute-start | bytes 368648 | tf_op jit(solution)/shard_map/ppermute | solution.py:25
  83.1 1.5 %collective-permute-start.13 = (s32[1]{0:T(128)}, s32[1]{0:T(128)}, u32[]{:S(2)}, u32[]{:S(2)}) collective-permute-start(s32[1]{0:T(128)} %bitcast.43), channel_id=1, source_target_pairs={{0,4},{4,0},{8,12},{12,8},{16,20},{20,16},{24,28},{28,24},{1,5},{5... | collective-permute-start | bytes 20 | tf_op jit(solution)/shard_map/ppermute | solution.py:25
  84.7 2.2 %collective-permute-done.13 = s32[1]{0:T(128)} collective-permute-done((s32[1]{0:T(128)}, s32[1]{0:T(128)}, u32[]{:S(2)}, u32[]{:S(2)}) %collective-permute-start.13) | collective-permute-done | bytes 36 | tf_op jit(solution)/shard_map/ppermute | solution.py:25
  88.1 3.0 %collective-permute-start.14 = (s32[1]{0:T(128)}, s32[1]{0:T(128)}, u32[]{:S(2)}, u32[]{:S(2)}) collective-permute-start(s32[1]{0:T(128)} %max.10), channel_id=1, source_target_pairs={{0,8},{4,12},{8,0},{12,4},{16,24},{20,28},{24,16},{28,20},{1,9},{5... | collective-permute-start | bytes 20 | tf_op jit(solution)/shard_map/ppermute | solution.py:25
  92.4 2.0 %fusion.53 = bf16[1,64,3072]{2,1,0:T(8,128)(2,1)} fusion(f32[64]{0:T(128)S(1)} %fusion.61, bf16[1,20,3072]{2,1,0:T(8,128)(2,1)} %collective-permute-done.12, f32[2,20,3072]{2,1,0:T(8,128)S(1)} %convert_add_fusion.1, s32[]{:T(128)} %select_n.105, s32[64]{0:T(128)S(1)} %broadcast_select_fusion.2, bf16[1,64,3072]{2,1,0:T(8,128)(2,1)S(1)} %copy-done.2), kind=kOutput, calls=%fused_computation.54 | convolution fusion | flops 8836352 | bytes 1205252 | tf_op jit(solution)/shard_map/dot_general | solution.py:21
  94.4 9.9 %collective-permute-done.19 = bf16[2,64,2048]{2,1,0:T(8,128)(2,1)} collective-permute-done((bf16[2,64,2048]{2,1,0:T(8,128)(2,1)}, bf16[2,64,2048]{2,1,0:T(8,128)(2,1)}, u32[]{:S(2)}, u32[]{:S(2)}) %collective-permute-start.19) | collective-permute-done | bytes 524320 | tf_op jit(solution)/shard_map/ppermute | solution.py:25
  104.2 4.1 %conditional.1 = (bf16[1,64,3072]{2,1,0:T(8,128)(2,1)S(1)}, bf16[1,2,80,2048]{3,2,1,0:T(8,128)(2,1)}) conditional(s32[]{:T(128)} %bitcast.44, (f32[2,20,3072]{2,1,0:T(8,128)S(1)}, s32[]{:T(128)}, f32[1,20,3072]{2,1,0:T(8,128)S(1)}, bf16[20,64]{1,0:T(8,128)(2,1)S(1)}, s32[17]{0:T(128)S(1)}, /*index=5*/bf16[2,64,2048]{2,1,0:T(8,128)(2,1)}) %tuple.16, ...), branch_computations={%region_6.7_spmd, %region_7.8_spmd} | conditional | flops 5045669888 | bytes 138009072 | solution.py:420
  104.5 3.7 %unpack.1 = bf16[2,80,2048]{2,1,0:T(8,128)(2,1)} custom-call(s32[17]{0:T(128)S(1)} %get-tuple-element.33.counts_ref, bf16[2,64,2048]{2,1,0:T(8,128)(2,1)} %get-tuple-element.34.packed_ref), custom_call_target="tpu_custom_call" | custom-call | tf_op jit(solution)/shard_map/cond/branch_0_fun/unpack/pallas_call | solution.py:395
  108.3 2.1 %copy.35 = bf16[1,2,80,2048]{3,2,1,0:T(8,128)(2,1)} copy(bf16[1,2,80,2048]{3,2,1,0:T(8,128)(2,1)} %get-tuple-element.85) | data formatting | bytes 1310720
  (69 shorter events, 16.3 us)
Async XLA Ops:
  6.1 14.6 %collective-permute-start.4 = (s32[2,4]{1,0:T(2,128)S(1)}, s32[2,4]{1,0:T(2,128)S(1)}, u32[]{:S(2)}, u32[]{:S(2)}) collective-permute-start(s32[2,4]{1,0:T(2,128)S(1)} %broadcast_select_fusion), channel_id=1, source_target_pairs={{0,16},{4,20},{8,24},{12,28},{16,0},{20,4},{24,8},{28,12},{1,17},{... | collective-permute-start | bytes 104 | tf_op jit(solution)/shard_map/ppermute | solution.py:25
  10.2 20.6 %collective-permute-start.7 = (bf16[1,20,3072]{2,1,0:T(8,128)(2,1)}, bf16[1,20,3072]{2,1,0:T(8,128)(2,1)S(1)}, u32[]{:S(2)}, u32[]{:S(2)}) collective-permute-start(bf16[1,20,3072]{2,1,0:T(8,128)(2,1)} %bitcast.135), channel_id=1, source_target_pairs={{0,2},{1,3},{2,0},{3,1},{4,6},{5,7},{6,4},{7,5},{8,10},{9,11},{10,... | collective-permute-start | bytes 368648 | tf_op jit(solution)/shard_map/ppermute | solution.py:25
  15.2 16.7 %collective-permute-start.9 = (bf16[1,20,3072]{2,1,0:T(8,128)(2,1)}, bf16[1,20,3072]{2,1,0:T(8,128)(2,1)S(1)}, u32[]{:S(2)}, u32[]{:S(2)}) collective-permute-start(bf16[1,20,3072]{2,1,0:T(8,128)(2,1)} %bitcast.133), channel_id=1, source_target_pairs={{0,2},{1,3},{2,0},{3,1},{4,6},{5,7},{6,4},{7,5},{8,10},{9,11},{10,... | collective-permute-start | bytes 368648 | tf_op jit(solution)/shard_map/ppermute | solution.py:25
  17.7 42.6 %collective-permute-start.15 = (bf16[2,32,2048]{2,1,0:T(8,128)(2,1)}, bf16[2,32,2048]{2,1,0:T(8,128)(2,1)S(1)}, u32[]{:S(2)}, u32[]{:S(2)}) collective-permute-start(bf16[2,32,2048]{2,1,0:T(8,128)(2,1)} %pack_early.1), channel_id=1, source_target_pairs={{0,16},{4,20},{8,24},{12,28},{16,0},{20,4},{24,8},{28,12},{1,17},{... | collective-permute-start | bytes 786440 | tf_op jit(solution)/shard_map/ppermute | solution.py:25
  20.7 3.7 %collective-permute-start.5 = (s32[2,2,4]{2,1,0:T(2,128)S(1)}, s32[2,2,4]{2,1,0:T(2,128)S(1)}, u32[]{:S(2)}, u32[]{:S(2)}) collective-permute-start(s32[2,2,4]{2,1,0:T(2,128)S(1)} %pad_add_fusion), channel_id=1, source_target_pairs={{0,2},{1,3},{2,0},{3,1},{4,6},{5,7},{6,4},{7,5},{8,10},{9,11},{10,... | collective-permute-start | bytes 200 | tf_op jit(solution)/shard_map/ppermute | solution.py:25
  24.3 1.2 %collective-permute-start.6 = (s32[2,2,4]{2,1,0:T(2,128)S(1)}, s32[2,2,4]{2,1,0:T(2,128)S(1)}, u32[]{:S(2)}, u32[]{:S(2)}) collective-permute-start(s32[2,2,4]{2,1,0:T(2,128)S(1)} %fusion.62), channel_id=1, source_target_pairs={{0,1},{1,0},{2,3},{3,2},{4,5},{5,4},{6,7},{7,6},{8,9},{9,8},{10,11... | collective-permute-start | bytes 200 | tf_op jit(solution)/shard_map/ppermute | solution.py:25
  27.8 32.5 %collective-permute-start.16 = (bf16[2,32,2048]{2,1,0:T(8,128)(2,1)}, bf16[2,32,2048]{2,1,0:T(8,128)(2,1)S(1)}, u32[]{:S(2)}, u32[]{:S(2)}) collective-permute-start(bf16[2,32,2048]{2,1,0:T(8,128)(2,1)} %pack_late.1), channel_id=1, source_target_pairs={{0,16},{4,20},{8,24},{12,28},{16,0},{20,4},{24,8},{28,12},{1,17},{... | collective-permute-start | bytes 786440 | tf_op jit(solution)/shard_map/ppermute | solution.py:25
  31.8 1.6 %collective-permute-start.8 = (bf16[2,20,3072]{2,1,0:T(8,128)(2,1)S(1)}, bf16[2,20,3072]{2,1,0:T(8,128)(2,1)S(1)}, u32[]{:S(2)}, u32[]{:S(2)}) collective-permute-start(bf16[2,20,3072]{2,1,0:T(8,128)(2,1)S(1)} %maximum_bitcast_fusion), channel_id=1, source_target_pairs={{0,1},{1,0},{2,3},{3,2},{4,5},{5,4},{6,7},{7,6},{8,9},{9,8},{10,11... | collective-permute-start | bytes 737288 | tf_op jit(solution)/shard_map/ppermute | solution.py:25
  32.8 1.8 %collective-permute-start.10 = (bf16[2,20,3072]{2,1,0:T(8,128)(2,1)S(1)}, bf16[2,20,3072]{2,1,0:T(8,128)(2,1)S(1)}, u32[]{:S(2)}, u32[]{:S(2)}) collective-permute-start(bf16[2,20,3072]{2,1,0:T(8,128)(2,1)S(1)} %maximum_bitcast_fusion.1), channel_id=1, source_target_pairs={{0,1},{1,0},{2,3},{3,2},{4,5},{5,4},{6,7},{7,6},{8,9},{9,8},{10,11... | collective-permute-start | bytes 737288 | tf_op jit(solution)/shard_map/ppermute | solution.py:25
  59.9 17.8 %collective-permute-start.11 = (bf16[2,20,3072]{2,1,0:T(8,128)(2,1)}, bf16[2,20,3072]{2,1,0:T(8,128)(2,1)S(1)}, u32[]{:S(2)}, u32[]{:S(2)}) collective-permute-start(bf16[2,20,3072]{2,1,0:T(8,128)(2,1)} %get-tuple-element.59), channel_id=1, source_target_pairs={{0,1},{1,0},{2,3},{3,2},{4,5},{5,4},{6,7},{7,6},{8,9},{9,8},{10,11... | collective-permute-start | bytes 737288 | tf_op jit(solution)/shard_map/ppermute | solution.py:25
  60.3 0.7 copy-start.6
  61.0 0.7 copy-start.7
  61.7 15.9 %copy-start.5 = (bf16[2,20,3072]{2,1,0:T(8,128)(2,1)S(1)}, bf16[2,20,3072]{2,1,0:T(8,128)(2,1)}, u32[]{:S(2)}) copy-start(bf16[2,20,3072]{2,1,0:T(8,128)(2,1)} %get-tuple-element.58) | copy-start | bytes 737284
  61.7 30.6 %copy-start.2 = (bf16[1,64,3072]{2,1,0:T(8,128)(2,1)S(1)}, bf16[1,64,3072]{2,1,0:T(8,128)(2,1)}, u32[]{:S(2)}) copy-start(bf16[1,64,3072]{2,1,0:T(8,128)(2,1)} %param.12) | copy-start | bytes 1179652
  61.7 42.5 %copy-start.1 = (bf16[1,2,80,2048]{3,2,1,0:T(8,128)(2,1)S(1)}, bf16[1,2,80,2048]{3,2,1,0:T(8,128)(2,1)}, u32[]{:S(2)}) copy-start(bf16[1,2,80,2048]{3,2,1,0:T(8,128)(2,1)} %param.21) | copy-start | bytes 1966084
  77.4 2.8 %collective-permute-start.17 = (bf16[2,20,3072]{2,1,0:T(8,128)(2,1)}, bf16[2,20,3072]{2,1,0:T(8,128)(2,1)S(1)}, u32[]{:S(2)}, u32[]{:S(2)}) collective-permute-start(bf16[2,20,3072]{2,1,0:T(8,128)(2,1)} %get-tuple-element.62), channel_id=1, source_target_pairs={{0,1},{1,0},{2,3},{3,2},{4,5},{5,4},{6,7},{7,6},{8,9},{9,8},{10,11... | collective-permute-start | bytes 737288 | tf_op jit(solution)/shard_map/ppermute | solution.py:25
  77.6 26.6 %collective-permute-start.19 = (bf16[2,64,2048]{2,1,0:T(8,128)(2,1)}, bf16[2,64,2048]{2,1,0:T(8,128)(2,1)}, u32[]{:S(2)}, u32[]{:S(2)}) collective-permute-start(bf16[2,64,2048]{2,1,0:T(8,128)(2,1)} %get-tuple-element.63), channel_id=1, source_target_pairs={{0,16},{4,20},{8,24},{12,28},{16,0},{20,4},{24,8},{28,12},{1,17},{... | collective-permute-start | bytes 1572872 | tf_op jit(solution)/shard_map/ppermute | solution.py:25
  78.4 13.9 %collective-permute-start.12 = (bf16[1,20,3072]{2,1,0:T(8,128)(2,1)}, bf16[1,20,3072]{2,1,0:T(8,128)(2,1)}, u32[]{:S(2)}, u32[]{:S(2)}) collective-permute-start(bf16[1,20,3072]{2,1,0:T(8,128)(2,1)} %dynamic-slice_convert_fusion.3), channel_id=1, source_target_pairs={{0,2},{1,3},{2,0},{3,1},{4,6},{5,7},{6,4},{7,5},{8,10},{9,11},{10,... | collective-permute-start | bytes 368648 | tf_op jit(solution)/shard_map/ppermute | solution.py:25
  81.9 10.4 %collective-permute-start.18 = (bf16[1,20,3072]{2,1,0:T(8,128)(2,1)}, bf16[1,20,3072]{2,1,0:T(8,128)(2,1)S(1)}, u32[]{:S(2)}, u32[]{:S(2)}) collective-permute-start(bf16[1,20,3072]{2,1,0:T(8,128)(2,1)} %dynamic-slice_convert_fusion.2), channel_id=1, source_target_pairs={{0,2},{1,3},{2,0},{3,1},{4,6},{5,7},{6,4},{7,5},{8,10},{9,11},{10,... | collective-permute-start | bytes 368648 | tf_op jit(solution)/shard_map/ppermute | solution.py:25
  83.1 3.7 %collective-permute-start.13 = (s32[1]{0:T(128)}, s32[1]{0:T(128)}, u32[]{:S(2)}, u32[]{:S(2)}) collective-permute-start(s32[1]{0:T(128)} %bitcast.43), channel_id=1, source_target_pairs={{0,4},{4,0},{8,12},{12,8},{16,20},{20,16},{24,28},{28,24},{1,5},{5... | collective-permute-start | bytes 20 | tf_op jit(solution)/shard_map/ppermute | solution.py:25
  88.1 3.6 %collective-permute-start.14 = (s32[1]{0:T(128)}, s32[1]{0:T(128)}, u32[]{:S(2)}, u32[]{:S(2)}) collective-permute-start(s32[1]{0:T(128)} %max.10), channel_id=1, source_target_pairs={{0,8},{4,12},{8,0},{12,4},{16,24},{20,28},{24,16},{28,20},{1,9},{5... | collective-permute-start | bytes 20 | tf_op jit(solution)/shard_map/ppermute | solution.py:25
  108.3 2.1 %copy-start.3 = (bf16[1,64,3072]{2,1,0:T(8,128)(2,1)}, bf16[1,64,3072]{2,1,0:T(8,128)(2,1)S(1)}, u32[]{:S(2)}) copy-start(bf16[1,64,3072]{2,1,0:T(8,128)(2,1)S(1)} %get-tuple-element.84) | copy-start | bytes 1179652
